TPU v7x, 256 devices: a whole 4x4x8 slice. The times are simulated.
256 devices in a mesh: aux: 2 (over core), row: 8 (over z), col: 16 (over x, y).
Axes of the slice: x: 4, y: 4, z: 8, core: 2. Of those that a mesh axis runs over, the one named last changes fastest.
Arguments:
- coulomb: bfloat16 [64, 2048, 2048], P('aux', 'row', 'col'), may hold values from -6 to 6
- occupied: bfloat16 [2048, 2048], P('row'), may hold values from -0.125 to 0.125
- virtual: bfloat16 [2048, 2048], P('row'), may hold values from -0.125 to 0.125
- tile_mask: int32 [16, 16], replicated, may hold values 0 or 1
Outputs:
- chi: float32 [64, 64], P('aux')
All inputs are finite; a program needn't handle non-finite values.
Results may differ from a plain program's by a relative error of at most 0.0042.
Values may be sent and summed in bfloat16 or wider, within the bound.
A program may use at most 128 MiB of HBM per device.

v0:
```python
import jax
import jax.numpy as jnp
from jax import lax
from jax.sharding import PartitionSpec as P

NAO = 2048
TILE = 128


def swapped(value, axis, apart):
    mask = 2**apart
    pairs = [(source, source ^ mask) for source in range(lax.axis_size(axis))]
    return lax.ppermute(value, axis, pairs)


def spread_density(local):
    cols = lax.axis_size("col")
    cores = lax.axis_size("aux")
    width = local.shape[1] // cols
    piece = lax.dynamic_slice_in_dim(local, lax.axis_index("col") * width, width, axis=1)
    column = lax.all_gather(piece, "row", axis=0, tiled=True)
    height = column.shape[0] // cores
    part = lax.dynamic_slice_in_dim(column, lax.axis_index("aux") * height, height, axis=0)
    rows = lax.all_gather(part, "col", axis=1, tiled=True)
    return lax.all_gather(rows, "aux", axis=0, tiled=True)


def shards(coulomb, occupied, virtual, tile_mask):
    rows = lax.axis_size("row")
    cols = lax.axis_size("col")
    pdev, mrow, ncol = coulomb.shape
    nao = mrow * rows
    row_idx = lax.axis_index("row")
    col_idx = lax.axis_index("col")
    aux_idx = lax.axis_index("aux")
    tiles_r = mrow // TILE
    tiles_c = ncol // TILE
    local_tiles = lax.dynamic_slice(
        tile_mask, (row_idx * tiles_r, col_idx * tiles_c), (tiles_r, tiles_c)
    )
    local_mask = jnp.repeat(jnp.repeat(local_tiles, TILE, axis=0), TILE, axis=1).astype(
        jnp.bfloat16
    )
    screened = coulomb * local_mask[None]
    moved = lax.all_to_all(screened, "row", split_axis=0, concat_axis=1, tiled=True)
    pieces = moved.shape[0]
    occ_all, virt_all = (spread_density(occupied), spread_density(virtual))
    half = jnp.einsum("ml,pmn->pln", occ_all, moved, preferred_element_type=jnp.float32).astype(
        jnp.bfloat16
    )
    jpart = mrow // cols
    shaped = half.reshape(pieces, rows, cols, jpart, ncol)
    spread = lax.all_to_all(shaped, "col", split_axis=2, concat_axis=4, tiled=True)
    spread = spread.reshape(pieces, rows * jpart, nao)
    dressed = jnp.einsum(
        "pln,ns->pls", spread, virt_all, preferred_element_type=jnp.float32
    ).astype(jnp.bfloat16)
    layered = dressed.reshape(pieces, rows, 1, jpart, cols, ncol)
    returned = lax.all_to_all(
        lax.all_to_all(layered, "row", split_axis=1, concat_axis=0, tiled=True),
        "col",
        split_axis=4,
        concat_axis=2,
        tiled=True,
    )
    aligned = returned.reshape(pdev, mrow, ncol)
    theirs = swapped(screened, "aux", 0)
    with_mine = jnp.einsum("pls,qls->pq", aligned, screened, preferred_element_type=jnp.float32)
    with_theirs = jnp.einsum("pls,qls->pq", aligned, theirs, preferred_element_type=jnp.float32)
    first_half = jnp.where(aux_idx == 0, with_mine, with_theirs)
    second_half = jnp.where(aux_idx == 0, with_theirs, with_mine)
    partial_chi = jnp.concatenate([first_half, second_half], axis=1)
    slots = lax.axis_size("aux")
    placed = jnp.zeros((slots,) + partial_chi.shape, partial_chi.dtype)
    placed = lax.dynamic_update_index_in_dim(placed, partial_chi, aux_idx, 0)
    total = lax.psum(placed, ("aux", "row", "col"))
    total_chi = lax.dynamic_index_in_dim(total, aux_idx, 0, keepdims=False)
    return total_chi / NAO


def solution(mesh):
    placed = (P("aux", "row", "col"), P("row", None), P("row", None), P())
    return jax.shard_map(
        shards, mesh=mesh, in_specs=placed, out_specs=P("aux", None), check_vma=False
    )
```

profile of v0, /device:TPU:1, one launch (start us, length us, event | category | flops | bytes accessed | tf_op | source)
XLA Modules:
  0.0 467.8 jit_solution(12967270680666020211)
XLA Ops:
  6.5 0.0 copy-start
  6.5 0.0 all-gather.5.cloned.1.call-start
  6.5 1.2 copy-done
  7.8 23.7 %all_gather.18 = bf16[2048,128]{1,0:T(8,128)(2,1)S(1)} all-gather(bf16[256,128]{1,0:T(8,128)(2,1)S(1)} %constant_dynamic-slice_fusion.3), channel_id=1, replica_groups=mesh['aux'=2,'row'=8,'col'=16] {'row'}, dimensions={0}, use_global_device_ids=true | all-gather | bytes 589824 | tf_op jit(solution)/shard_map/all_gather | solution.py:21
  31.5 0.7 constant_dynamic-slice_fusion.2
  32.2 0.0 all-gather.5.cloned.1.call-update
  32.3 0.0 all-gather.9.cloned.1.call-start
  32.3 0.9 constant_dynamic-slice_fusion.1
  33.2 19.8 %all_gather.21 = bf16[2048,128]{1,0:T(8,128)(2,1)S(1)} all-gather(bf16[256,128]{1,0:T(8,128)(2,1)S(1)} %constant_dynamic-slice_fusion.1), channel_id=1, replica_groups=mesh['aux'=2,'row'=8,'col'=16] {'row'}, dimensions={0}, use_global_device_ids=true | all-gather | bytes 589824 | tf_op jit(solution)/shard_map/all_gather | solution.py:21
  53.0 0.7 constant_dynamic-slice_fusion
  53.7 0.0 all-gather.9.cloned.1.call-update
  53.7 0.0 all-gather.7.cloned.1.call-start
  53.8 45.8 %all-gather.5.cloned.1.call-done = bf16[1024,2048]{1,0:T(8,128)(2,1)} async-done(((bf16[1024,128]{1,0:T(8,128)(2,1)}), bf16[1024,2048]{1,0:T(8,128)(2,1)}) %all-gather.5.cloned.1.call-update) | async-done | bytes 4194320 | tf_op jit(solution)/shard_map/all_gather | solution.py:24
  99.5 0.0 all-gather.7.cloned.1.call-update
  99.6 0.0 all-gather.11.cloned.1.call-start
  99.6 64.4 %all-gather.9.cloned.1.call-done = bf16[1024,2048]{1,0:T(8,128)(2,1)} async-done(((bf16[1024,128]{1,0:T(8,128)(2,1)}), bf16[1024,2048]{1,0:T(8,128)(2,1)}) %all-gather.9.cloned.1.call-update) | async-done | bytes 4194320 | tf_op jit(solution)/shard_map/all_gather | solution.py:24
  164.0 0.0 all-gather.11.cloned.1.call-update
  164.0 0.9 fusion.14
  164.9 0.1 broadcast_bitcast_fusion
  165.0 2.8 copy_multiply_fusion
  167.7 0.8 copy.15
  168.6 55.1 %all_to_all.66 = bf16[32,256,128]{2,1,0:T(8,128)(2,1)} all-to-all(bf16[32,256,128]{2,1,0:T(8,128)(2,1)S(1)} %copy.15), channel_id=1, replica_groups=mesh['aux'=2,'row'=8,'col'=16] {'row'}, dimensions={0} | all-to-all | bytes 4194304 | tf_op jit(solution)/shard_map/all_to_all | solution.py:45
  223.7 4.5 copy.16
  228.2 4.2 all_to_all.51
  232.4 0.0 all-gather.7.cloned.1.call-done
  232.4 9.8 %fusion.10 = bf16[4,2048,128]{1,2,0:T(8,128)(2,1)} fusion(bf16[4,2048,128]{1,2,0:T(8,128)(2,1)} %all_to_all.51, bf16[2048,2048]{1,0:T(8,128)(2,1)} %all-gather.7.cloned.1.call-done), kind=kOutput, calls=%fused_computation.6 | convolution fusion | flops 4296015872 | bytes 12582912 | tf_op jit(solution)/shard_map/ml,pmn->pln/dot_general | solution.py:48
  242.3 3.9 copy.17
  246.2 2.2 copy.18
  248.4 28.7 %all_to_all.67 = bf16[4,8,16,16,128]{4,3,1,0,2:T(8,128)(2,1)S(1)} all-to-all(bf16[4,8,16,16,128]{4,3,1,0,2:T(8,128)(2,1)S(1)} %copy.18), channel_id=1, replica_groups=mesh['aux'=2,'row'=8,'col'=16] {'col'}, dimensions={2} | all-to-all | bytes 4194304 | tf_op jit(solution)/shard_map/all_to_all | solution.py:53
  277.1 3.8 copy.19
  280.8 4.2 reshape.37
  285.0 8.5 %fusion.7 = bf16[4,128,2048]{2,1,0:T(8,128)(2,1)S(1)} fusion(bf16[4,128,2048]{2,1,0:T(8,128)(2,1)} %reshape.37, bf16[2048,2048]{1,0:T(8,128)(2,1)} %all-gather.11.cloned.1.call-done), kind=kOutput, calls=%fused_computation.5 | convolution fusion | flops 4296015872 | bytes 12582912 | tf_op jit(solution)/shard_map/pln,ns->pls/dot_general | solution.py:55
  293.6 0.6 copy.23
  294.2 0.6 copy.20
  294.8 51.9 %all_to_all.68 = bf16[4,8,1,16,16,128]{5,4,3,0,2,1:T(8,128)(2,1)S(1)} all-to-all(bf16[4,8,1,16,16,128]{5,4,3,0,2,1:T(8,128)(2,1)S(1)} %copy.20), channel_id=1, replica_groups=mesh['aux'=2,'row'=8,'col'=16] {'row'}, dimensions={1} | all-to-all | bytes 4194304 | tf_op jit(solution)/shard_map/all_to_all | solution.py:60
  346.6 1.9 copy.21
  348.5 5.3 %all-to-all-start.3 = ((bf16[32,1,1,16,16,128]{5,3,0,2,1,4:T(8,128)(2,1)}), bf16[32,1,1,16,16,128]{5,3,0,2,1,4:T(8,128)(2,1)}, u32[]{:S(2)}, u32[]{:S(2)}) async-start(bf16[32,1,1,16,16,128]{5,3,0,2,1,4:T(8,128)(2,1)} %copy.21), calls=%async_computation.3 | async-start | bytes 4194304 | tf_op jit(solution)/shard_map/all_to_all | solution.py:59
  353.8 4.7 collective-permute-start
  358.5 19.6 %all-to-all-done.3 = bf16[32,1,1,16,16,128]{5,3,0,2,1,4:T(8,128)(2,1)} async-done(((bf16[32,1,1,16,16,128]{5,3,0,2,1,4:T(8,128)(2,1)}), bf16[32,1,1,16,16,128]{5,3,0,2,1,4:T(8,128)(2,1)}, u32[]{:S(2)}, u32[]{:S(2)}) %all-to-all-start.3) | async-done | bytes 2097184 | tf_op jit(solution)/shard_map/all_to_all | solution.py:59
  378.0 2.1 copy.22
  380.2 0.0 copy-start.1
  380.2 0.7 convolution_bitcast_fusion.1
  380.8 0.0 collective-permute-done
  380.9 2.3 broadcast_select_fusion.1
  383.2 0.1 fusion.13
  383.3 77.4 %psum.7 = f32[2,32,64]{2,1,0:T(8,128)S(1)} all-reduce(f32[2,32,64]{2,1,0:T(8,128)S(1)} %fusion.13), channel_id=1, replica_groups=mesh['aux'=2,'row'=8,'col'=16] {'aux','row','col'}, use_global_device_ids=true, to_apply=%region_0.1 | all-reduce | flops 4096 | bytes 32768 | tf_op jit(solution)/shard_map/psum | solution.py:76
  460.7 0.6 multiply_bitcast_fusion
  461.3 0.0 copy-done.1
  (3 shorter events, 0.0 us)
Async XLA Ops:
  6.5 1.2 copy-start
  6.5 93.0 %all-gather.5.cloned.1.call-start = ((), (), s32[]{:S(2)}) async-start(), calls=%async_computation.4 | async-start | bytes 4456448 | tf_op jit(solution)/shard_map/all_gather | solution.py:24
  32.3 131.7 %all-gather.9.cloned.1.call-start = ((), (), s32[]{:S(2)}) async-start(), calls=%async_computation.6 | async-start | bytes 4456448 | tf_op jit(solution)/shard_map/all_gather | solution.py:24
  53.7 178.7 %all-gather.7.cloned.1.call-start = ((), (), s32[]{:S(2)}) async-start(), calls=%async_computation.5 | async-start | bytes 12582912 | tf_op jit(solution)/shard_map/all_gather | solution.py:25
  99.6 185.5 %all-gather.11.cloned.1.call-start = ((), (), s32[]{:S(2)}) async-start(), calls=%async_computation.7 | async-start | bytes 12582912 | tf_op jit(solution)/shard_map/all_gather | solution.py:25
  348.5 29.5 %all-to-all-start.3 = ((bf16[32,1,1,16,16,128]{5,3,0,2,1,4:T(8,128)(2,1)}), bf16[32,1,1,16,16,128]{5,3,0,2,1,4:T(8,128)(2,1)}, u32[]{:S(2)}, u32[]{:S(2)}) async-start(bf16[32,1,1,16,16,128]{5,3,0,2,1,4:T(8,128)(2,1)} %copy.21), calls=%async_computation.3 | async-start | bytes 4194304 | tf_op jit(solution)/shard_map/all_to_all | solution.py:59
  353.8 27.0 %collective-permute-start = (bf16[32,256,128]{2,0,1:T(8,128)(2,1)S(1)}, bf16[32,256,128]{2,0,1:T(8,128)(2,1)}, u32[]{:S(2)}, u32[]{:S(2)}) collective-permute-start(bf16[32,256,128]{2,0,1:T(8,128)(2,1)S(1)} %copy_multiply_fusion), channel_id=1, source_target_pairs={{0,128},{128,0},{1,129},{129,1},{2,130},{130,2},{3,131},{131,3},{4... | collective-permute-start | bytes 6291464 | tf_op jit(solution)/shard_map/ppermute | solution.py:13
  380.2 81.1 %copy-start.1 = (bf16[256,2048]{1,0:T(8,128)(2,1)S(1)}, bf16[256,2048]{1,0:T(8,128)(2,1)}, u32[]{:S(2)}) copy-start(bf16[256,2048]{1,0:T(8,128)(2,1)} %param.5) | copy-start | bytes 3145732
Sparse Core Ops, SparseCore 0:
  32.4 67.0 all-gather.4
  101.9 62.0 all-gather.8
  165.8 26.2 all-gather.6
  193.7 26.4 all-gather.10
where the time goes:
time: 469 us; the launch traced here: 468 us
  blocking collectives  257 us (55%)
  waiting for transfers between devices  130 us (28%)
  local copies, waits for them, and re-layouts  32.5 us (7%)
  matrix products  21.3 us (5%)
  between operations  13.2 us (3%)
  starting transfers between devices  10.1 us (2%)
    all_gather x2, waiting for transfers between devices, spread_density(): rows = lax.all_gather(part, 'col', axis=1, tiled=True)  110 us
    psum x1, blocking collectives, shards(): total = lax.psum(placed, ('aux', 'row', 'col'))  77.4 us
    all_to_all x1, blocking collectives, shards(): lax.all_to_all(screened, 'row', split_axis=0, concat_axis=1, tiled=True)  55.1 us
    all_to_all x1, blocking collectives, shards(): lax.all_to_all(layered, 'row', split_axis=1, concat_axis=0, tiled=True)  51.9 us
    all_gather x2, blocking collectives, spread_density(): column = lax.all_gather(piece, 'row', axis=0, tiled=True)  43.5 us
    all_to_all x1, blocking collectives, shards(): lax.all_to_all(shaped, 'col', split_axis=2, concat_axis=4, tiled=True)  28.7 us
    all_to_all x1, waiting for transfers between devices, shards(): lax.all_to_all(lax.all_to_all(layered, 'row', split_axis=1, concat_axis=0...  19.6 us
    dot_general x1, matrix products, shards(): jnp.einsum('ml,pmn->pln', occ_all, moved, preferred_element_type=jnp.floa...  9.83 us
  transfers between devices with their start and end apart: 6, of which 3 were waited for; matrix products, arithmetic and copies ran while one was open for 8% of the time, Pallas kernels for 0%

commit v1 on v0

--- a/solution.py
+++ b/solution.py
@@ -22,7 +22,9 @@
     height = column.shape[0] // cores
     part = lax.dynamic_slice_in_dim(column, lax.axis_index("aux") * height, height, axis=0)
     rows = lax.all_gather(part, "col", axis=1, tiled=True)
-    return lax.all_gather(rows, "aux", axis=0, tiled=True)
+    return jnp.concatenate(
+        lax.all_to_all(jnp.stack([rows] * lax.axis_size("aux")), "aux", 0, 0), axis=0
+    )
 
 
 def shards(coulomb, occupied, virtual, tile_mask):

time: 469 us -> 402 us (0.86)
  waiting for transfers between devices: 130 us -> 49.1 us
  blocking collectives: 257 us -> 240 us
  starting transfers between devices: 10.1 us -> 26.4 us
  other arithmetic: 4.33 us -> 19.2 us
    all_gather x2, waiting for transfers between devices: 110 us -> 0.95 us  [spread_density(): rows = lax.all_gather(part, 'col', axis=1, tiled=True)]
    all_to_all x0 -> x2, waiting for transfers between devices: none -> 20.9 us  [the longest x1 20.9 us: shards(): lax.all_to_all(shaped, 'col', split_axis=2, concat_axis=4, tiled=True)]
    all_to_all x0 -> x2, starting transfers between devices: none -> 16.3 us  [the longest x1 9.52 us: spread_density(): lax.all_to_all(jnp.stack([rows] * lax.axis_size('aux')), 'aux', 0, 0)]
    another operation x0 -> x2, other arithmetic: none -> 14.9 us  [spread_density(): jnp.stack([rows] * lax.axis_size('aux'))]
    all_to_all x1, blocking collectives: 55.1 us -> 42.7 us  [shards(): lax.all_to_all(screened, 'row', split_axis=0, concat_axis=1, tiled=True)]
    all_to_all x1, waiting for transfers between devices: 19.6 us -> 27.3 us  [shards(): lax.all_to_all(lax.all_to_all(layered, 'row', split_axis=1, concat_axis=0...]
  transfers between devices with their start and end apart: 6 -> 6, of which waited for: 3 -> 3; matrix products, arithmetic and copies ran while one was open for 8% -> 13% of each run, Pallas kernels for 0% -> 0%
where the time goes in v1:
time: 402 us; the launch traced here: 401 us
  blocking collectives  240 us (60%)
  waiting for transfers between devices  49.1 us (12%)
  local copies, waits for them, and re-layouts  35.3 us (9%)
  starting transfers between devices  26.4 us (7%)
  other arithmetic  19.2 us (5%)
  matrix products  17.3 us (4%)
  between operations  13.5 us (3%)
    psum x1, blocking collectives, shards(): total = lax.psum(placed, ('aux', 'row', 'col'))  73.9 us
    all_to_all x1, blocking collectives, shards(): lax.all_to_all(layered, 'row', split_axis=1, concat_axis=0, tiled=True)  54.2 us
    all_gather x2, blocking collectives, spread_density(): column = lax.all_gather(piece, 'row', axis=0, tiled=True)  43.5 us
    all_to_all x1, blocking collectives, shards(): lax.all_to_all(screened, 'row', split_axis=0, concat_axis=1, tiled=True)  42.7 us
    all_to_all x1, waiting for transfers between devices, shards(): lax.all_to_all(lax.all_to_all(layered, 'row', split_axis=1, concat_axis=0...  27.3 us
    all_to_all x1, blocking collectives, spread_density(): lax.all_to_all(jnp.stack([rows] * lax.axis_size('aux')), 'aux', 0, 0)  25.9 us
    all_to_all x1, waiting for transfers between devices, shards(): lax.all_to_all(shaped, 'col', split_axis=2, concat_axis=4, tiled=True)  20.9 us
    another operation x2, other arithmetic, spread_density(): jnp.stack([rows] * lax.axis_size('aux'))  14.9 us
  transfers between devices with their start and end apart: 6, of which 3 were waited for; matrix products, arithmetic and copies ran while one was open for 13% of the time, Pallas kernels for 0%

profile of v1, /device:TPU:1, one launch (start us, length us, event | category | flops | bytes accessed | tf_op | source)
XLA Modules:
  0.0 401.1 jit_solution(16841177090500621050)
XLA Ops:
  6.5 0.0 copy-start
  6.5 0.0 all-gather.3.cloned.1.call-start
  6.5 1.2 copy-done
  7.8 23.7 %all_gather.12 = bf16[2048,128]{1,0:T(8,128)(2,1)S(1)} all-gather(bf16[256,128]{1,0:T(8,128)(2,1)S(1)} %constant_dynamic-slice_fusion.3), channel_id=1, replica_groups=mesh['aux'=2,'row'=8,'col'=16] {'row'}, dimensions={0}, use_global_device_ids=true | all-gather | bytes 589824 | tf_op jit(solution)/shard_map/all_gather | solution.py:21
  31.5 0.7 constant_dynamic-slice_fusion.2
  32.2 0.0 all-gather.3.cloned.1.call-update
  32.3 0.0 all-gather.5.cloned.1.call-start
  32.3 0.9 constant_dynamic-slice_fusion.1
  33.2 19.8 %all_gather.14 = bf16[2048,128]{1,0:T(8,128)(2,1)S(1)} all-gather(bf16[256,128]{1,0:T(8,128)(2,1)S(1)} %constant_dynamic-slice_fusion.1), channel_id=1, replica_groups=mesh['aux'=2,'row'=8,'col'=16] {'row'}, dimensions={0}, use_global_device_ids=true | all-gather | bytes 589824 | tf_op jit(solution)/shard_map/all_gather | solution.py:21
  53.0 0.7 constant_dynamic-slice_fusion
  53.7 0.0 all-gather.5.cloned.1.call-update
  53.7 0.9 fusion.2
  54.6 0.1 broadcast_bitcast_fusion
  54.7 2.8 copy_multiply_fusion
  57.4 0.8 copy.15
  58.3 42.7 %all_to_all.76 = bf16[32,256,128]{2,1,0:T(8,128)(2,1)} all-to-all(bf16[32,256,128]{2,1,0:T(8,128)(2,1)S(1)} %copy.15), channel_id=1, replica_groups=mesh['aux'=2,'row'=8,'col'=16] {'row'}, dimensions={0} | all-to-all | bytes 4194304 | tf_op jit(solution)/shard_map/all_to_all | solution.py:47
  101.0 4.5 %copy.16 = bf16[8,4,256,128]{2,0,3,1:T(8,128)(2,1)} copy(bf16[8,4,256,128]{3,2,1,0:T(8,128)(2,1)} %bitcast.61) | data formatting | bytes 4194304 | tf_op jit(solution)/shard_map/all_to_all | solution.py:47
  105.5 4.2 %all_to_all.57 = bf16[4,2048,128]{1,2,0:T(8,128)(2,1)} reshape(bf16[4,8,256,128]{2,1,3,0:T(8,128)(2,1)} %bitcast.62) | data formatting | bytes 4194304 | tf_op jit(solution)/shard_map/all_to_all | solution.py:47
  109.7 7.4 %pad_maximum_fusion = bf16[2,1024,2048]{2,1,0:T(8,128)(2,1)} fusion(bf16[1,1024,2048]{2,1,0:T(8,128)(2,1)} %bitcast.67), kind=kLoop, calls=%fused_computation | loop fusion | flops 4194304 | bytes 12582912 | tf_op jit(solution)/shard_map/stack | solution.py:26
  117.1 25.9 %all_to_all.77 = bf16[2,1024,2048]{2,1,0:T(8,128)(2,1)S(1)} all-to-all(bf16[2,1024,2048]{2,1,0:T(8,128)(2,1)} %pad_maximum_fusion), channel_id=1, replica_groups=mesh['aux'=2,'row'=8,'col'=16] {'aux'}, dimensions={0} | all-to-all | bytes 16777216 | tf_op jit(solution)/shard_map/all_to_all | solution.py:26
  143.0 0.0 copy-done.2
  143.0 5.8 %fusion = bf16[4,2048,128]{1,2,0:T(8,128)(2,1)} fusion(bf16[4,2048,128]{1,2,0:T(8,128)(2,1)S(1)} %copy-done.2, bf16[2048,2048,1]{1,0,2:T(8,128)(2,1)S(1)} %bitcast.60), kind=kOutput, calls=%fused_computation.4 | convolution fusion | flops 4296015872 | bytes 12582912 | tf_op jit(solution)/shard_map/ml,pmn->pln/dot_general | solution.py:50
  148.8 4.0 copy.17
  152.8 3.5 copy.18
  156.3 6.8 %all-to-all-start.2 = ((bf16[4,8,16,16,128]{4,3,1,0,2:T(8,128)(2,1)}), bf16[4,8,16,16,128]{4,3,1,0,2:T(8,128)(2,1)}, u32[]{:S(2)}, u32[]{:S(2)}) async-start(bf16[4,8,16,16,128]{4,3,1,0,2:T(8,128)(2,1)} %copy.18), calls=%async_computation.2 | async-start | bytes 4194304 | tf_op jit(solution)/shard_map/all_to_all | solution.py:55
  163.0 1.0 all-gather.5.cloned.1.call-done
  164.0 7.4 %pad_maximum_fusion.1 = bf16[2,1024,2048]{2,1,0:T(8,128)(2,1)} fusion(bf16[1,1024,2048]{2,1,0:T(8,128)(2,1)} %bitcast.66), kind=kLoop, calls=%fused_computation.1 | loop fusion | flops 4194304 | bytes 12582912 | tf_op jit(solution)/shard_map/stack | solution.py:26
  171.4 20.9 %all-to-all-done.2 = bf16[4,8,16,16,128]{4,3,1,0,2:T(8,128)(2,1)} async-done(((bf16[4,8,16,16,128]{4,3,1,0,2:T(8,128)(2,1)}), bf16[4,8,16,16,128]{4,3,1,0,2:T(8,128)(2,1)}, u32[]{:S(2)}, u32[]{:S(2)}) %all-to-all-start.2) | async-done | bytes 2097184 | tf_op jit(solution)/shard_map/all_to_all | solution.py:55
  192.3 9.5 %all-to-all-start.3 = ((bf16[2,1024,2048]{2,1,0:T(8,128)(2,1)}), bf16[2,1024,2048]{2,1,0:T(8,128)(2,1)}, u32[]{:S(2)}, u32[]{:S(2)}) async-start(bf16[2,1024,2048]{2,1,0:T(8,128)(2,1)} %pad_maximum_fusion.1), calls=%async_computation.3 | async-start | bytes 16777216 | tf_op jit(solution)/shard_map/all_to_all | solution.py:26
  201.8 5.3 %copy.19 = bf16[4,8,1,16,16,128]{5,4,3,1,0,2:T(8,128)(2,1)} copy(bf16[4,8,1,16,16,128]{5,3,1,0,4,2:T(8,128)(2,1)} %bitcast.9) | data formatting | bytes 4194304 | tf_op jit(solution)/shard_map/all_to_all | solution.py:55
  207.2 4.1 %reshape.44 = bf16[4,128,2048]{2,1,0:T(8,128)(2,1)} reshape(bf16[4,8,1,16,16,128]{5,4,3,1,0,2:T(8,128)(2,1)} %copy.19) | data formatting | bytes 4194304 | tf_op jit(solution)/shard_map/reshape | solution.py:56
  211.3 0.0 all-to-all-done.3
  211.3 8.5 %convolution_convert_fusion = bf16[4,128,2048]{2,1,0:T(8,128)(2,1)S(1)} fusion(bf16[4,128,2048]{2,1,0:T(8,128)(2,1)} %reshape.44, bf16[2048,2048,1]{1,0,2:T(8,128)(2,1)} %bitcast.12), kind=kOutput, calls=%fused_computation.2 | convolution fusion | flops 4296015872 | bytes 12582912 | tf_op jit(solution)/shard_map/pln,ns->pls/dot_general | solution.py:57
  219.9 0.6 copy.23
  220.5 0.6 copy.20
  221.1 54.2 %all_to_all.78 = bf16[4,8,1,16,16,128]{5,4,3,0,2,1:T(8,128)(2,1)S(1)} all-to-all(bf16[4,8,1,16,16,128]{5,4,3,0,2,1:T(8,128)(2,1)S(1)} %copy.20), channel_id=1, replica_groups=mesh['aux'=2,'row'=8,'col'=16] {'row'}, dimensions={1} | all-to-all | bytes 4194304 | tf_op jit(solution)/shard_map/all_to_all | solution.py:62
  275.3 1.9 copy.21
  277.2 9.1 %all-to-all-start.5 = ((bf16[32,1,1,16,16,128]{5,3,0,2,1,4:T(8,128)(2,1)}), bf16[32,1,1,16,16,128]{5,3,0,2,1,4:T(8,128)(2,1)}, u32[]{:S(2)}, u32[]{:S(2)}) async-start(bf16[32,1,1,16,16,128]{5,3,0,2,1,4:T(8,128)(2,1)} %copy.21), calls=%async_computation.5 | async-start | bytes 4194304 | tf_op jit(solution)/shard_map/all_to_all | solution.py:61
  286.3 1.0 collective-permute-start
  287.3 27.3 %all-to-all-done.5 = bf16[32,1,1,16,16,128]{5,3,0,2,1,4:T(8,128)(2,1)} async-done(((bf16[32,1,1,16,16,128]{5,3,0,2,1,4:T(8,128)(2,1)}), bf16[32,1,1,16,16,128]{5,3,0,2,1,4:T(8,128)(2,1)}, u32[]{:S(2)}, u32[]{:S(2)}) %all-to-all-start.5) | async-done | bytes 2097184 | tf_op jit(solution)/shard_map/all_to_all | solution.py:61
  314.6 2.1 copy.22
  316.7 0.0 copy-start.1
  316.7 0.7 convolution_bitcast_fusion.1
  317.4 0.0 collective-permute-done
  317.4 2.3 broadcast_select_fusion.1
  319.7 0.1 fusion.1
  319.8 73.9 %psum.7 = f32[2,32,64]{2,1,0:T(8,128)S(1)} all-reduce(f32[2,32,64]{2,1,0:T(8,128)S(1)} %fusion.1), channel_id=1, replica_groups=mesh['aux'=2,'row'=8,'col'=16] {'aux','row','col'}, use_global_device_ids=true, to_apply=%region_0.1 | all-reduce | flops 4096 | bytes 32768 | tf_op jit(solution)/shard_map/psum | solution.py:78
  393.7 0.6 multiply_bitcast_fusion
  (5 shorter events, 0.0 us)
Async XLA Ops:
  6.5 1.2 copy-start
  6.5 103.1 %all-gather.3.cloned.1.call-start = ((), (), s32[]{:S(2)}) async-start(), calls=%async_computation.6 | async-start | bytes 4456448 | tf_op jit(solution)/shard_map/all_gather | solution.py:24
  32.3 131.7 %all-gather.5.cloned.1.call-start = ((), (), s32[]{:S(2)}) async-start(), calls=%async_computation.7 | async-start | bytes 4456448 | tf_op jit(solution)/shard_map/all_gather | solution.py:24
  117.1 25.9 %copy-start.2 = (bf16[4,2048,128]{1,2,0:T(8,128)(2,1)S(1)}, bf16[4,2048,128]{1,2,0:T(8,128)(2,1)}, u32[]{:S(2)}) copy-start(bf16[4,2048,128]{1,2,0:T(8,128)(2,1)} %all_to_all.57) | copy-start | bytes 6291460
  156.3 36.0 %all-to-all-start.2 = ((bf16[4,8,16,16,128]{4,3,1,0,2:T(8,128)(2,1)}), bf16[4,8,16,16,128]{4,3,1,0,2:T(8,128)(2,1)}, u32[]{:S(2)}, u32[]{:S(2)}) async-start(bf16[4,8,16,16,128]{4,3,1,0,2:T(8,128)(2,1)} %copy.18), calls=%async_computation.2 | async-start | bytes 4194304 | tf_op jit(solution)/shard_map/all_to_all | solution.py:55
  192.3 19.0 %all-to-all-start.3 = ((bf16[2,1024,2048]{2,1,0:T(8,128)(2,1)}), bf16[2,1024,2048]{2,1,0:T(8,128)(2,1)}, u32[]{:S(2)}, u32[]{:S(2)}) async-start(bf16[2,1024,2048]{2,1,0:T(8,128)(2,1)} %pad_maximum_fusion.1), calls=%async_computation.3 | async-start | bytes 16777216 | tf_op jit(solution)/shard_map/all_to_all | solution.py:26
  277.2 37.4 %all-to-all-start.5 = ((bf16[32,1,1,16,16,128]{5,3,0,2,1,4:T(8,128)(2,1)}), bf16[32,1,1,16,16,128]{5,3,0,2,1,4:T(8,128)(2,1)}, u32[]{:S(2)}, u32[]{:S(2)}) async-start(bf16[32,1,1,16,16,128]{5,3,0,2,1,4:T(8,128)(2,1)} %copy.21), calls=%async_computation.5 | async-start | bytes 4194304 | tf_op jit(solution)/shard_map/all_to_all | solution.py:61
  286.3 31.1 %collective-permute-start = (bf16[32,256,128]{2,0,1:T(8,128)(2,1)S(1)}, bf16[32,256,128]{2,0,1:T(8,128)(2,1)}, u32[]{:S(2)}, u32[]{:S(2)}) collective-permute-start(bf16[32,256,128]{2,0,1:T(8,128)(2,1)S(1)} %copy_multiply_fusion), channel_id=1, source_target_pairs={{0,128},{128,0},{1,129},{129,1},{2,130},{130,2},{3,131},{131,3},{4... | collective-permute-start | bytes 6291464 | tf_op jit(solution)/shard_map/ppermute | solution.py:13
  316.7 77.6 %copy-start.1 = (bf16[256,2048]{1,0:T(8,128)(2,1)S(1)}, bf16[256,2048]{1,0:T(8,128)(2,1)}, u32[]{:S(2)}) copy-start(bf16[256,2048]{1,0:T(8,128)(2,1)} %param.5) | copy-start | bytes 3145732
Sparse Core Ops, SparseCore 0:
  32.4 67.0 all-gather.2
  101.9 62.0 all-gather.4
